TPU v7x, 256 devices: a whole 4x4x8 slice. The times are simulated.
256 devices in a mesh: seq: 32 (over y_lo, z, core), head: 8 (over x, y_hi).
Axes of the slice: x: 4, y: 4 (y_hi: 2, y_lo: 2; y = y_hi * 2 + y_lo), z: 8, core: 2. Of those that a mesh axis runs over, the one named last changes fastest.
Arguments:
- queries: bfloat16 [12288, 3072], P('seq', 'head'), may hold values from -56 to 56, as said below
- keys: bfloat16 [12288, 3072], P('seq', 'head'), may hold values from -4 to 4, as said below
- values: bfloat16 [12288, 3072], P('seq', 'head'), may hold values from -6 to 6
- out_weight: bfloat16 [3072, 3072], P('head'), may hold values from -0.109375 to 0.109375
- residual: bfloat16 [12288, 3072], P(('seq', 'head')), may hold values from -6 to 6
- gate: float32 [3072], replicated, may hold values from 0.5 to 2
Outputs:
- mixed: bfloat16 [12288, 3072], P(('seq', 'head'))
Inputs may be any that keep to these rules, and one draw needn't show every extreme that they name: `queries`: query entries of the attention. `keys`: key entries of the attention.
All inputs are finite; a program needn't handle non-finite values.
Results may differ from a plain program's by a relative error of at most 0.0075.
Values may be sent and summed in bfloat16 or wider, within the bound.
No kernel may reach another device: no remote copies, remote signals or barrier semaphores. Data moves between devices by JAX's collectives and lax.ppermute only.
A program may use at most 192 MiB of HBM per device.

v0:
```python
import jax
import jax.numpy as jnp
from jax import lax
from jax.sharding import PartitionSpec as P

HD = 128


def local(queries, keys, values, out_weight, residual, gate):
    tok_rows = queries.shape[0]
    heads_here = queries.shape[1] // HD
    scale = 1.0 / HD**0.5
    query_heads = queries.reshape(tok_rows, heads_here, HD)
    gathered = (
        lax.all_gather(keys, "seq", axis=0, tiled=True),
        lax.all_gather(values, "seq", axis=0, tiled=True),
    )
    running_max = jnp.full((heads_here, tok_rows), -1e30, jnp.float32)
    key_piece = gathered[0].reshape(-1, heads_here, HD)
    value_piece = gathered[1].reshape(-1, heads_here, HD)
    scores = (
        jnp.einsum("qhd,khd->hqk", query_heads, key_piece, preferred_element_type=jnp.float32)
        * scale
    )
    new_max = jnp.maximum(running_max, jnp.max(scores, axis=-1))
    expd = jnp.exp(scores - new_max[:, :, None])
    new_total = jnp.sum(expd, axis=-1)
    probs = expd.astype(jnp.bfloat16)
    added = jnp.einsum("hqk,khd->qhd", probs, value_piece, preferred_element_type=jnp.float32)
    final_state = (new_max, new_total, added)
    running_max, running_total, summed = final_state
    attention = (summed / jnp.transpose(running_total)[:, :, None]).astype(jnp.bfloat16)
    attention = attention.reshape(tok_rows, heads_here * HD)
    projected = lax.psum_scatter(
        jnp.dot(attention, out_weight, preferred_element_type=jnp.float32).astype(jnp.bfloat16),
        "head",
        scatter_dimension=0,
        tiled=True,
    ).astype(jnp.float32)
    return (residual.astype(jnp.float32) + gate * projected).astype(jnp.bfloat16)


def solution(mesh):
    placed = (
        P("seq", "head"),
        P("seq", "head"),
        P("seq", "head"),
        P("head", None),
        P(("seq", "head"), None),
        P(),
    )
    return jax.shard_map(
        local, mesh=mesh, in_specs=placed, out_specs=P(("seq", "head"), None), check_vma=False
    )
```

profile of v0, /device:TPU:2, one launch (start us, length us, event | category | flops | bytes accessed | tf_op | source)
XLA Modules:
  0.0 287.6 jit_solution(7186178622220679946)
XLA Ops:
  6.5 0.0 copy-start
  6.5 0.0 all-gather.3.cloned.1.call-start
  6.5 2.0 copy.10
  8.5 0.0 all-gather.3.cloned.1.call-update
  8.6 0.0 all-gather.5.cloned.1.call-start
  8.6 0.7 all-gather.5.cloned.1.call-update
  9.3 0.0 reduce-scatter.2.cloned.1.call-start
  9.4 1.2 copy.9
  10.5 75.2 %all-gather.3.cloned.1.call-done = bf16[12288,384]{0,1:T(8,128)(2,1)} async-done(((bf16[384,384]{0,1:T(8,128)(2,1)}), bf16[12288,384]{0,1:T(8,128)(2,1)}) %all-gather.3.cloned.1.call-update) | async-done | bytes 9437200 | tf_op jit(solution)/shard_map/all_gather | solution.py:15
  85.7 24.7 %multiply_reduce_fusion = (f32[3,384]{1,0:T(4,128)S(1)}, f32[3,384,12288]{2,1,0:T(8,128)}) fusion(bf16[384,3,128]{0,2,1:T(8,128)(2,1)S(1)} %bitcast.19, bf16[12288,3,128]{0,2,1:T(8,128)(2,1)} %bitcast.17), kind=kOutput, calls=%fused_computation.1 | convolution fusion | flops 3652189184 | bytes 66359808 | tf_op jit(solution)/shard_map/qhd,khd->hqk/dot_general | solution.py:22
  110.4 19.4 %fusion = f32[3,384]{1,0:T(4,128)S(1)} fusion(f32[3,384,12288]{2,1,0:T(8,128)} %get-tuple-element.6, f32[3,384]{1,0:T(4,128)S(1)} %broadcast_maximum_fusion), kind=kLoop, calls=%fused_computation.2 | loop fusion | flops 42466176 | bytes 56632320 | tf_op jit(solution)/shard_map/reduce_sum | solution.py:27
  129.8 29.4 %all-gather.5.cloned.1.call-done = bf16[12288,384]{1,0:T(8,128)(2,1)} async-done(((bf16[384,384]{1,0:T(8,128)(2,1)}), bf16[12288,384]{1,0:T(8,128)(2,1)}) %all-gather.5.cloned.1.call-update) | async-done | bytes 9437200 | tf_op jit(solution)/shard_map/all_gather | solution.py:16
  159.2 12.6 %copy.13 = bf16[12288,384]{0,1:T(8,128)(2,1)} copy(bf16[12288,384]{1,0:T(8,128)(2,1)} %all-gather.5.cloned.1.call-done) | data formatting | bytes 18874368 | tf_op jit(solution)/shard_map/all_gather | solution.py:16
  171.8 0.0 copy-start.1
  171.8 0.0 copy-start.2
  171.8 22.7 %fusion.12 = bf16[384,3,128]{0,2,1:T(8,128)(2,1)S(1)} fusion(bf16[12288,3,128]{0,2,1:T(8,128)(2,1)} %bitcast.16, f32[3,384,12288]{2,1,0:T(8,128)} %get-tuple-element.6, f32[3,384]{1,0:T(4,128)S(1)} %broadcast_maximum_fusion, f32[384,3]{0,1:T(4,128)S(1)} %bitcast.20), kind=kOutput, calls=%fused_computation.10 | convolution fusion | flops 3666640896 | bytes 66364416 | tf_op jit(solution)/shard_map/hqk,khd->qhd/dot_general | solution.py:29
  194.4 0.0 copy-done
  194.5 2.9 convolution_convert_fusion
  197.3 0.0 reduce-scatter.2.cloned.1.call-update
  197.3 82.0 %reduce-scatter.2.cloned.1.call-done = bf16[48,3072]{1,0:T(8,128)(2,1)} async-done(((bf16[384,3072]{1,0:T(8,128)(2,1)}), bf16[48,3072]{1,0:T(8,128)(2,1)}) %reduce-scatter.2.cloned.1.call-update) | async-done | bytes 294928 | tf_op jit(solution)/shard_map/reduce_scatter | solution.py:34
  279.3 0.0 copy-done.1
  279.3 0.0 copy-done.2
  279.3 1.8 add_convert_fusion
  (1 shorter events, 0.0 us)
Async XLA Ops:
  6.5 187.9 %copy-start = (bf16[384,3072]{1,0:T(8,128)(2,1)S(1)}, bf16[384,3072]{1,0:T(8,128)(2,1)}, u32[]{:S(2)}) copy-start(bf16[384,3072]{1,0:T(8,128)(2,1)} %param.9) | copy-start | bytes 7077892
  6.5 79.2 %all-gather.3.cloned.1.call-start = ((), (), s32[]{:S(2)}) async-start(), calls=%async_computation.1 | async-start | bytes 9732096 | tf_op jit(solution)/shard_map/all_gather | solution.py:15
  8.6 150.6 %all-gather.5.cloned.1.call-start = ((), (), s32[]{:S(2)}) async-start(), calls=%async_computation.2 | async-start | bytes 9732096 | tf_op jit(solution)/shard_map/all_gather | solution.py:16
  9.3 270.0 %reduce-scatter.2.cloned.1.call-start = ((), (), s32[]{:S(2)}) async-start(), calls=%async_computation.3 | async-start | bytes 2654208 | tf_op jit(solution)/shard_map/reduce_scatter | solution.py:34
  171.8 107.5 %copy-start.1 = (bf16[48,3072]{1,0:T(8,128)(2,1)S(1)}, bf16[48,3072]{1,0:T(8,128)(2,1)}, u32[]{:S(2)}) copy-start(bf16[48,3072]{1,0:T(8,128)(2,1)} %param.10) | copy-start | bytes 884740
  171.8 107.5 %copy-start.2 = (f32[3072]{0:T(1024)S(1)}, f32[3072]{0:T(1024)}, u32[]{:S(2)}) copy-start(f32[3072]{0:T(1024)} %param.11) | copy-start | bytes 36868
Sparse Core Ops, SparseCore 0:
  9.1 76.5 all-gather.2
  87.5 71.5 all-gather.4
  197.5 81.8 reduce-scatter.1
where the time goes:
time: 288 us
  waiting for transfers between devices  187 us (65%)
  matrix products  50.2 us (17%)
  other arithmetic  21.2 us (7%)
  local copies, waits for them, and re-layouts  15.8 us (5%)
  between operations  13.1 us (5%)
    reduce_scatter x1, waiting for transfers between devices, local(): lax.psum_scatter(jnp.dot(attention, out_weight, preferred_element_type=jn...  82 us
    all_gather x1, waiting for transfers between devices, local(): lax.all_gather(keys, 'seq', axis=0, tiled=True)  75.2 us
    all_gather x1, waiting for transfers between devices, local(): lax.all_gather(values, 'seq', axis=0, tiled=True)  29.4 us
    dot_general x1, matrix products, local(): jnp.einsum('qhd,khd->hqk', query_heads, key_piece, preferred_element_type...  24.7 us
    dot_general x1, matrix products, local(): jnp.einsum('hqk,khd->qhd', probs, value_piece, preferred_element_type=jnp...  22.7 us
    reduce_sum x1, other arithmetic, local(): new_total = jnp.sum(expd, axis=-1)  19.4 us
    all_gather x1, local copies, waits for them, and re-layouts, local(): lax.all_gather(values, 'seq', axis=0, tiled=True)  12.6 us
  transfers between devices with their start and end apart: 3, of which 3 were waited for; matrix products, arithmetic and copies ran while one was open for 16% of the time, Pallas kernels for 0%

commit v1 on v0

--- a/solution.py
+++ b/solution.py
@@ -13,7 +13,9 @@
     query_heads = queries.reshape(tok_rows, heads_here, HD)
     gathered = (
         lax.all_gather(keys, "seq", axis=0, tiled=True),
-        lax.all_gather(values, "seq", axis=0, tiled=True),
+        jnp.concatenate(
+            lax.all_to_all(jnp.stack([values] * lax.axis_size("seq")), "seq", 0, 0), axis=0
+        ),
     )
     running_max = jnp.full((heads_here, tok_rows), -1e30, jnp.float32)
     key_piece = gathered[0].reshape(-1, heads_here, HD)

time: 288 us -> 449 us (1.56)
  waiting for transfers between devices: 187 us -> 319 us
  local copies, waits for them, and re-layouts: 15.8 us -> 35.4 us
  starting transfers between devices: 0.08 us -> 10 us
    all_gather x1, waiting for transfers between devices: 75.2 us -> 188 us  [local(): lax.all_gather(keys, 'seq', axis=0, tiled=True)]
    all_to_all x0 -> x1, waiting for transfers between devices: none -> 41.8 us  [local(): lax.all_to_all(jnp.stack([values] * lax.axis_size('seq')), 'seq', 0, 0)]
    all_gather x1 -> x0, waiting for transfers between devices: 29.4 us -> none  [local(): lax.all_gather(values, 'seq', axis=0, tiled=True)]
    another operation x0 -> x2, local copies, waits for them, and re-layouts: none -> 19.2 us  [the longest x1 14.1 us: local(): value_piece = gathered[1].reshape(-1, heads_here, HD)]
    all_to_all x0 -> x1, local copies, waits for them, and re-layouts: none -> 12.8 us  [local(): lax.all_to_all(jnp.stack([values] * lax.axis_size('seq')), 'seq', 0, 0)]
    all_gather x1 -> x0, local copies, waits for them, and re-layouts: 12.6 us -> none  [local(): lax.all_gather(values, 'seq', axis=0, tiled=True)]
    all_to_all x0 -> x1, starting transfers between devices: none -> 9.98 us  [local(): lax.all_to_all(jnp.stack([values] * lax.axis_size('seq')), 'seq', 0, 0)]
    reduce_scatter x1, waiting for transfers between devices: 82 us -> 88.8 us  [local(): lax.psum_scatter(jnp.dot(attention, out_weight, preferred_element_type=jn...]
  transfers between devices with their start and end apart: 3 -> 3, of which waited for: 3 -> 3; matrix products, arithmetic and copies ran while one was open for 16% -> 7% of each run, Pallas kernels for 0% -> 0%
where the time goes in v1:
time: 449 us; the launch traced here: 448 us
  waiting for transfers between devices  319 us (71%)
  matrix products  50 us (11%)
  local copies, waits for them, and re-layouts  35.4 us (8%)
  other arithmetic  20.4 us (5%)
  between operations  13.5 us (3%)
  starting transfers between devices  10 us (2%)
    all_gather x1, waiting for transfers between devices, local(): lax.all_gather(keys, 'seq', axis=0, tiled=True)  188 us
    reduce_scatter x1, waiting for transfers between devices, local(): lax.psum_scatter(jnp.dot(attention, out_weight, preferred_element_type=jn...  88.8 us
    all_to_all x1, waiting for transfers between devices, local(): lax.all_to_all(jnp.stack([values] * lax.axis_size('seq')), 'seq', 0, 0)  41.8 us
    dot_general x1, matrix products, local(): jnp.einsum('qhd,khd->hqk', query_heads, key_piece, preferred_element_type...  24.2 us
    dot_general x1, matrix products, local(): jnp.einsum('hqk,khd->qhd', probs, value_piece, preferred_element_type=jnp...  22.9 us
    reduce_sum x1, other arithmetic, local(): new_total = jnp.sum(expd, axis=-1)  18.6 us
    another operation x1, local copies, waits for them, and re-layouts, local(): value_piece = gathered[1].reshape(-1, heads_here, HD)  14.1 us
    all_to_all x1, local copies, waits for them, and re-layouts, local(): lax.all_to_all(jnp.stack([values] * lax.axis_size('seq')), 'seq', 0, 0)  12.8 us
  transfers between devices with their start and end apart: 3, of which 3 were waited for; matrix products, arithmetic and copies ran while one was open for 7% of the time, Pallas kernels for 0%

profile of v1, /device:TPU:2, one launch (start us, length us, event | category | flops | bytes accessed | tf_op | source)
XLA Modules:
  0.0 448.2 jit_solution(4885025949913287093)
XLA Ops:
  6.5 0.0 copy-start
  6.5 0.0 copy-start.2
  6.5 0.0 all-gather.2.cloned.1.call-start
  6.5 2.0 copy.15
  8.5 0.0 all-gather.2.cloned.1.call-update
  8.6 1.2 copy.18
  9.7 5.1 %stack.2 = bf16[32,384,384]{1,2,0:T(8,128)(2,1)} broadcast(bf16[384,384]{0,1:T(8,128)(2,1)S(1)} %copy.18), dimensions={1,2} | broadcast | bytes 9732096 | tf_op jit(solution)/shard_map/stack | solution.py:17
  14.8 10.0 %all-to-all-start = ((bf16[32,384,384]{1,2,0:T(8,128)(2,1)}), bf16[32,384,384]{1,2,0:T(8,128)(2,1)}, u32[]{:S(2)}, u32[]{:S(2)}) async-start(bf16[32,384,384]{1,2,0:T(8,128)(2,1)} %stack.2), calls=%async_computation | async-start | bytes 18874368 | tf_op jit(solution)/shard_map/all_to_all | solution.py:17
  24.8 0.0 reduce-scatter.2.cloned.1.call-start
  24.9 0.0 copy-done.2
  24.9 0.2 copy.14
  25.1 188.3 %all-gather.2.cloned.1.call-done = bf16[12288,384]{0,1:T(8,128)(2,1)} async-done(((bf16[384,384]{0,1:T(8,128)(2,1)}), bf16[12288,384]{0,1:T(8,128)(2,1)}) %all-gather.2.cloned.1.call-update) | async-done | bytes 9437200 | tf_op jit(solution)/shard_map/all_gather | solution.py:15
  213.4 24.2 %multiply_reduce_fusion = (f32[3,384]{1,0:T(4,128)S(1)}, f32[3,384,12288]{2,1,0:T(8,128)}) fusion(bf16[384,3,128]{0,2,1:T(8,128)(2,1)S(1)} %bitcast.19, bf16[12288,3,128]{0,2,1:T(8,128)(2,1)} %bitcast.17), kind=kOutput, calls=%fused_computation.1 | convolution fusion | flops 3652189184 | bytes 66359808 | tf_op jit(solution)/shard_map/qhd,khd->hqk/dot_general | solution.py:24
  237.6 41.8 %all-to-all-done = bf16[32,384,384]{1,2,0:T(8,128)(2,1)} async-done(((bf16[32,384,384]{1,2,0:T(8,128)(2,1)}), bf16[32,384,384]{1,2,0:T(8,128)(2,1)}, u32[]{:S(2)}, u32[]{:S(2)}) %all-to-all-start) | async-done | bytes 9437216 | tf_op jit(solution)/shard_map/all_to_all | solution.py:17
  279.5 12.8 %copy.19 = bf16[32,384,384]{1,0,2:T(8,128)(2,1)} copy(bf16[32,384,384]{1,2,0:T(8,128)(2,1)} %all-to-all-done) | data formatting | bytes 18874368 | tf_op jit(solution)/shard_map/all_to_all | solution.py:17
  292.2 14.1 %reshape_reshape.3 = bf16[12288,3,128]{0,2,1:T(8,128)(2,1)} reshape(bf16[32,384,384]{1,0,2:T(8,128)(2,1)} %copy.19) | data formatting | bytes 18874368 | tf_op jit(solution)/shard_map/reshape;reshape | solution.py:22
  306.4 18.6 %fusion = f32[3,384]{1,0:T(4,128)S(1)} fusion(f32[3,384,12288]{2,1,0:T(8,128)} %get-tuple-element.6, f32[3,384]{1,0:T(4,128)S(1)} %broadcast_maximum_fusion), kind=kLoop, calls=%fused_computation.2 | loop fusion | flops 42466176 | bytes 56632320 | tf_op jit(solution)/shard_map/reduce_sum | solution.py:29
  325.0 0.0 copy-start.1
  325.0 0.0 copy-start.3
  325.0 22.9 %fusion.12 = bf16[384,3,128]{0,2,1:T(8,128)(2,1)S(1)} fusion(bf16[12288,3,128]{0,2,1:T(8,128)(2,1)} %reshape_reshape.3, f32[3,384,12288]{2,1,0:T(8,128)} %get-tuple-element.6, f32[3,384]{1,0:T(4,128)S(1)} %broadcast_maximum_fusion, f32[384,3]{0,1:T(4,128)S(1)} %bitcast.20), kind=kOutput, calls=%fused_computation.10 | convolution fusion | flops 3666640896 | bytes 66364416 | tf_op jit(solution)/shard_map/hqk,khd->qhd/dot_general | solution.py:31
  347.9 0.0 copy-done
  347.9 2.9 convolution_convert_fusion
  350.8 0.0 reduce-scatter.2.cloned.1.call-update
  350.8 88.8 %reduce-scatter.2.cloned.1.call-done = bf16[48,3072]{1,0:T(8,128)(2,1)} async-done(((bf16[384,3072]{1,0:T(8,128)(2,1)}), bf16[48,3072]{1,0:T(8,128)(2,1)}) %reduce-scatter.2.cloned.1.call-update) | async-done | bytes 294928 | tf_op jit(solution)/shard_map/reduce_scatter | solution.py:36
  439.6 0.0 copy-done.1
  439.6 0.0 copy-done.3
  439.6 1.8 add_convert_fusion
  (1 shorter events, 0.0 us)
Async XLA Ops:
  6.5 341.4 %copy-start = (bf16[384,3072]{1,0:T(8,128)(2,1)S(1)}, bf16[384,3072]{1,0:T(8,128)(2,1)}, u32[]{:S(2)}) copy-start(bf16[384,3072]{1,0:T(8,128)(2,1)} %param.9) | copy-start | bytes 7077892
  6.5 18.3 %copy-start.2 = (bf16[384,384]{1,0:T(8,128)(2,1)S(1)}, bf16[384,384]{1,0:T(8,128)(2,1)}, u32[]{:S(2)}) copy-start(bf16[384,384]{1,0:T(8,128)(2,1)} %param.6) | copy-start | bytes 884740
  6.5 206.9 %all-gather.2.cloned.1.call-start = ((), (), s32[]{:S(2)}) async-start(), calls=%async_computation.2 | async-start | bytes 9732096 | tf_op jit(solution)/shard_map/all_gather | solution.py:15
  14.8 264.6 %all-to-all-start = ((bf16[32,384,384]{1,2,0:T(8,128)(2,1)}), bf16[32,384,384]{1,2,0:T(8,128)(2,1)}, u32[]{:S(2)}, u32[]{:S(2)}) async-start(bf16[32,384,384]{1,2,0:T(8,128)(2,1)} %stack.2), calls=%async_computation | async-start | bytes 18874368 | tf_op jit(solution)/shard_map/all_to_all | solution.py:17
  24.8 414.8 %reduce-scatter.2.cloned.1.call-start = ((), (), s32[]{:S(2)}) async-start(), calls=%async_computation.3 | async-start | bytes 2654208 | tf_op jit(solution)/shard_map/reduce_scatter | solution.py:36
  325.0 114.6 %copy-start.1 = (bf16[48,3072]{1,0:T(8,128)(2,1)S(1)}, bf16[48,3072]{1,0:T(8,128)(2,1)}, u32[]{:S(2)}) copy-start(bf16[48,3072]{1,0:T(8,128)(2,1)} %param.10) | copy-start | bytes 884740
  325.0 114.6 %copy-start.3 = (f32[3072]{0:T(1024)S(1)}, f32[3072]{0:T(1024)}, u32[]{:S(2)}) copy-start(f32[3072]{0:T(1024)} %param.11) | copy-start | bytes 36868
Sparse Core Ops, SparseCore 0:
  9.1 204.2 all-gather.1
  350.9 88.6 reduce-scatter.1
